TPU v7x, 512 devices: a whole 4x8x8 slice. The times are simulated.
512 devices in a mesh: row: 8 (over y), col: 64 (over z, x, core).
Axes of the slice: x: 4, y: 8, z: 8, core: 2. Of those that a mesh axis runs over, the one named last changes fastest.
Arguments:
- ppmi: bfloat16 [4096, 128256], P('row', 'col'), may hold values from -12000 to 12000
- basis: bfloat16 [256, 128256], P(None, 'col'), may hold values from -10 to 10
Outputs:
- left_basis: bfloat16 [256, 4096], P(None, 'row')
- right_basis: bfloat16 [256, 128256], P(None, 'col')
All inputs are finite; a program needn't handle non-finite values.
Results may differ from a plain program's by a relative error of at most 0.0045.
Values may be sent and summed in bfloat16 or wider, within the bound.
A program may use at most 128 MiB of HBM per device.

v0:
```python
import jax
import jax.numpy as jnp
from jax import lax
from jax.sharding import Mesh
from jax.sharding import PartitionSpec as P

COL = ("col_0", "col_1", "col_2")


def in_blocks(array, dim, peers):
    before, after = (array.shape[:dim], array.shape[dim + 1 :])
    return jnp.moveaxis(array.reshape(*before, peers, -1, *after), dim, 0)


def sum_at_owner(array, axis, dim):
    peers = lax.axis_size(axis)
    pieces = lax.all_to_all(in_blocks(array, dim, peers), axis, 0, 0, tiled=True)
    return jnp.sum(pieces, axis=0)


def summed_rows(array, axes, dim):
    far, near = axes
    pieces = in_blocks(array, dim, lax.axis_size(far))
    nearer = sum_at_owner(pieces, near, dim + 1)
    arrived = lax.all_to_all(nearer, far, split_axis=0, concat_axis=0, tiled=True)
    return arrived.sum(axis=0)


def rows_for(lines, peers):
    spare = -len(lines) % peers
    return jnp.pad(lines, [(0, spare)] + [(0, 0)] * (lines.ndim - 1))


def copy_for_each(array, axis):
    peers = lax.axis_size(axis)
    return lax.all_to_all(
        jnp.broadcast_to(array[None], (peers, *array.shape)), axis, 0, 0, tiled=True
    )


def joined_along(pieces, dim):
    shape = list(pieces.shape[1:])
    shape[dim] *= pieces.shape[0]
    return jnp.moveaxis(pieces, 0, dim).reshape(shape)


def gathered_by_axis(array, axes, dim):
    far, near = axes
    pieces = copy_for_each(copy_for_each(array, far), near)
    return joined_along(pieces.swapaxes(0, 1).reshape(-1, *array.shape), dim)


def nested_sum(array, axes):
    lines = array.reshape(-1, array.shape[-1])
    own = summed_rows(rows_for(lines, lax.axis_size(axes[0]) * lax.axis_size(axes[1])), axes, 0)
    whole = gathered_by_axis(own, axes, 0)
    return whole[: len(lines)].reshape(array.shape)


def of_everyone(array, axis):
    everything = copy_for_each(array, axis)
    return jnp.sum(everything, axis=0)


def local_gram(block):
    return jnp.dot(block, block.T, precision=lax.Precision.HIGHEST)


def solve_rows(gram, block):
    lower = jnp.linalg.cholesky(gram)
    solved = lax.linalg.triangular_solve(lower, block, left_side=True, lower=True)
    return solved.astype(jnp.bfloat16)


def local(ppmi, basis):
    rows_total = ppmi.shape[0] * lax.axis_size("row")
    cols_total = ppmi.shape[1] * lax.axis_size(COL)
    basis_now = basis
    left = None
    partial_value = lax.dot_general(
        basis_now, ppmi, (((1,), (1,)), ((), ())), preferred_element_type=jnp.float32
    )
    y_total = nested_sum(partial_value, (("col_0", "col_1"), "col_2"))
    gram_left = of_everyone(local_gram(y_total), "row") / rows_total
    left = solve_rows(gram_left, y_total)
    z_part = jnp.dot(left, ppmi, preferred_element_type=jnp.float32)
    z_total = lax.psum(z_part, "row")
    gram_right = nested_sum(local_gram(z_total), (("col_0", "col_1"), "col_2")) / cols_total
    basis_now = solve_rows(gram_right, z_total)
    return (left, basis_now)


def solution(mesh):
    split = Mesh(
        mesh.devices.reshape(mesh.shape["row"], 8, 4, 2), ("row", "col_0", "col_1", "col_2")
    )
    placed = (P("row", COL), P(None, COL))
    return jax.shard_map(
        local,
        mesh=split,
        in_specs=placed,
        out_specs=(P(None, "row"), P(None, COL)),
        check_vma=False,
    )
```

profile of v0, /device:TPU:1, one launch (start us, length us, event | category | flops | bytes accessed | tf_op | source)
XLA Modules:
  0.0 395.1 jit_solution(5545338627759966449)
XLA Ops:
  7.2 1.6 copy-done
  8.7 1.9 fusion.18
  10.8 0.8 copy.40
  11.7 10.4 %all-to-all-start = ((f32[2,32,4,512]{3,2,1,0:T(4,128)}), f32[2,32,4,512]{3,2,1,0:T(4,128)S(1)}, u32[]{:S(2)}, u32[]{:S(2)}) async-start(f32[2,32,4,512]{3,2,1,0:T(4,128)} %bitcast.70), calls=%async_computation | async-start | bytes 1048576 | tf_op jit(solution)/shard_map/all_to_all | solution.py:17
  22.0 1.4 all-to-all-done
  23.6 18.9 %all_to_all.49 = f32[32,4,512]{2,1,0:T(4,128)S(1)} all-to-all(f32[32,4,512]{2,1,0:T(4,128)S(1)} %reduce_sum.45), channel_id=1, replica_groups=mesh['row'=8,'col_0'=8,'col_1'=4,'col_2'=2] {'col_0','col_1'}, dimensions={0} | all-to-all | bytes 524288 | tf_op jit(solution)/shard_map/all_to_all | solution.py:25
  42.6 15.0 %all_to_all.45 = f32[32,4,512]{2,1,0:T(4,128)S(1)} all-to-all(f32[32,4,512]{2,1,0:T(4,128)S(1)} %broadcast_in_dim.10), channel_id=1, replica_groups=mesh['row'=8,'col_0'=8,'col_1'=4,'col_2'=2] {'col_0','col_1'}, dimensions={0} | all-to-all | bytes 524288 | tf_op jit(solution)/shard_map/all_to_all | solution.py:36
  57.7 7.1 %all_to_all.46 = f32[2,32,4,512]{3,2,1,0:T(4,128)S(1)} all-to-all(f32[2,32,4,512]{3,2,1,0:T(4,128)S(1)} %broadcast_in_dim.11), channel_id=1, replica_groups=mesh['row'=8,'col_0'=8,'col_1'=4,'col_2'=2] {'col_2'}, dimensions={0} | all-to-all | bytes 1048576 | tf_op jit(solution)/shard_map/all_to_all | solution.py:36
  64.7 0.9 copy.27
  65.6 1.2 reshape_reshape.11
  66.8 0.6 fusion.19
  67.5 1.5 broadcast_in_dim.12
  68.9 6.8 %all-to-all-start.4 = ((f32[8,256,256]{2,1,0:T(8,128)}), f32[8,256,256]{2,1,0:T(8,128)}, u32[]{:S(2)}, u32[]{:S(2)}) async-start(f32[8,256,256]{2,1,0:T(8,128)} %broadcast_in_dim.12), calls=%async_computation.4 | async-start | bytes 4194304 | tf_op jit(solution)/shard_map/all_to_all | solution.py:36
  76.4 47.8 %all-to-all-done.4 = f32[8,256,256]{2,1,0:T(8,128)} async-done(((f32[8,256,256]{2,1,0:T(8,128)}), f32[8,256,256]{2,1,0:T(8,128)}, u32[]{:S(2)}, u32[]{:S(2)}) %all-to-all-start.4) | async-done | bytes 2097184 | tf_op jit(solution)/shard_map/all_to_all | solution.py:36
  124.2 1.8 reduce_sum.47
  126.3 11.7 %cholesky.130 = f32[128,128]{1,0:T(8,128)S(1)} custom-call(f32[128,128]{1,0:T(8,128)S(1)} %cholesky.194), custom_call_target="Cholesky" | custom-call | tf_op jit(solution)/shard_map/jit(cholesky)/cholesky | solution.py:70
  138.1 9.8 %custom-call.17 = f32[1,128,128]{1,2,0:T(8,128)S(1)} custom-call(f32[1,128,128]{2,1,0:T(8,128)S(1)} %get-tuple-element.48), custom_call_target="InvertDiagBlocksLowerTriangular" | custom-call | tf_op jit(solution)/shard_map/jit(cholesky)/cholesky | solution.py:70
  148.4 11.7 %cholesky.147 = f32[128,128]{1,0:T(8,128)S(1)} custom-call(f32[128,128]{1,0:T(8,128)S(1)} %convolution_subtract_fusion.3), custom_call_target="Cholesky" | custom-call | tf_op jit(solution)/shard_map/jit(cholesky)/cholesky | solution.py:70
  160.1 0.7 compare_reduce_fusion.2
  162.2 4.6 %while.2 = (s32[]{:T(128)}, f32[256,256]{1,0:T(8,128)S(1)}, s32[2,2]{1,0:T(2,128)S(1)}, f32[2,128,128]{2,1,0:T(8,128)S(1)}, s32[]{:T(128)}) while((s32[]{:T(128)}, f32[256,256]{1,0:T(8,128)S(1)}, s32[2,2]{1,0:T(2,128)S(1)}, f32[2,128,128]{2,1,0:T(8,128)S(1)}, s32[]{:T(128)}) %tuple.48), condition=%wide.while_cond, body=%wide.while_body.sunk | while | flops 2 | bytes 131189 | solution.py:71
  162.8 0.7 fusion.41
  163.5 1.3 bitcast_dynamic-update-slice_fusion.4
  164.8 0.7 fusion.41
  165.5 1.3 bitcast_dynamic-update-slice_fusion.4
  166.8 19.7 %custom-call.14 = f32[2,128,128]{1,2,0:T(8,128)S(1)} custom-call(f32[2,128,128]{2,1,0:T(8,128)S(1)} %get-tuple-element.10), custom_call_target="InvertDiagBlocksLowerTriangular" | custom-call | tf_op jit(solution)/shard_map/triangular_solve | solution.py:71
  187.3 0.4 convolution_convert_fusion.1
  187.8 2.0 fusion.20
  189.8 77.2 %all-reduce.3.cloned.1.call-done = f32[256,2004]{0,1:T(8,128)} async-done(((f32[256,2004]{0,1:T(8,128)}), f32[256,2004]{0,1:T(8,128)}) %all-reduce.3.cloned.1.call-update) | async-done | bytes 2052112 | tf_op jit(solution)/shard_map/psum | solution.py:87
  267.0 5.7 %fusion.21 = f32[256,256]{1,0:T(8,128)S(1)} fusion(f32[256,2004]{0,1:T(8,128)} %all-reduce.3.cloned.1.call-done), kind=kOutput, calls=%fused_computation.63 | convolution fusion | flops 1576009728 | bytes 2314240 | tf_op jit(solution)/shard_map/dot_general | solution.py:66
  272.8 7.7 %all_to_all.47 = f32[2,32,4,256]{3,2,1,0:T(4,128)S(1)} all-to-all(f32[2,32,4,256]{3,2,1,0:T(4,128)S(1)} %bitcast.86), channel_id=1, replica_groups=mesh['row'=8,'col_0'=8,'col_1'=4,'col_2'=2] {'col_2'}, dimensions={0} | all-to-all | bytes 524288 | tf_op jit(solution)/shard_map/all_to_all | solution.py:17
  280.5 19.1 %all_to_all.50 = f32[32,4,256]{2,1,0:T(4,128)S(1)} all-to-all(f32[32,4,256]{2,1,0:T(4,128)S(1)} %reduce_sum.48), channel_id=1, replica_groups=mesh['row'=8,'col_0'=8,'col_1'=4,'col_2'=2] {'col_0','col_1'}, dimensions={0} | all-to-all | bytes 262144 | tf_op jit(solution)/shard_map/all_to_all | solution.py:25
  299.7 13.0 %all_to_all.51 = f32[32,4,256]{2,1,0:T(4,128)S(1)} all-to-all(f32[32,4,256]{2,1,0:T(4,128)S(1)} %broadcast_in_dim.14), channel_id=1, replica_groups=mesh['row'=8,'col_0'=8,'col_1'=4,'col_2'=2] {'col_0','col_1'}, dimensions={0} | all-to-all | bytes 262144 | tf_op jit(solution)/shard_map/all_to_all | solution.py:36
  312.7 6.6 %all_to_all.48 = f32[2,32,4,256]{3,2,1,0:T(4,128)S(1)} all-to-all(f32[2,32,4,256]{3,2,1,0:T(4,128)S(1)} %broadcast_in_dim.15), channel_id=1, replica_groups=mesh['row'=8,'col_0'=8,'col_1'=4,'col_2'=2] {'col_2'}, dimensions={0} | all-to-all | bytes 524288 | tf_op jit(solution)/shard_map/all_to_all | solution.py:36
  319.8 11.7 %cholesky.164 = f32[128,128]{1,0:T(8,128)S(1)} custom-call(f32[128,128]{1,0:T(8,128)S(1)} %cholesky.197), custom_call_target="Cholesky" | custom-call | tf_op jit(solution)/shard_map/jit(cholesky)/cholesky | solution.py:70
  331.5 0.7 compare_reduce_fusion.1
  332.2 9.8 %custom-call.18 = f32[1,128,128]{1,2,0:T(8,128)S(1)} custom-call(f32[1,128,128]{2,1,0:T(8,128)S(1)} %get-tuple-element.44), custom_call_target="InvertDiagBlocksLowerTriangular" | custom-call | tf_op jit(solution)/shard_map/jit(cholesky)/cholesky | solution.py:70
  342.5 11.7 %cholesky.181 = f32[128,128]{1,0:T(8,128)S(1)} custom-call(f32[128,128]{1,0:T(8,128)S(1)} %convolution_subtract_fusion.2), custom_call_target="Cholesky" | custom-call | tf_op jit(solution)/shard_map/jit(cholesky)/cholesky | solution.py:70
  354.3 0.6 compare_reduce_fusion
  356.2 4.1 %while.3 = (s32[]{:T(128)}, f32[256,256]{1,0:T(8,128)S(1)}, s32[2,2]{1,0:T(2,128)S(1)}, f32[2,128,128]{2,1,0:T(8,128)S(1)}, s32[]{:T(128)}) while((s32[]{:T(128)}, f32[256,256]{1,0:T(8,128)S(1)}, s32[2,2]{1,0:T(2,128)S(1)}, f32[2,128,128]{2,1,0:T(8,128)S(1)}, s32[]{:T(128)}) %tuple.56), condition=%wide.while_cond.1, body=%wide.while_body.1.sunk | while | flops 2 | bytes 131189 | solution.py:71
  356.3 0.7 fusion.42
  356.9 1.3 bitcast_dynamic-update-slice_fusion.5
  358.3 0.7 fusion.42
  359.0 1.3 bitcast_dynamic-update-slice_fusion.5
  360.3 19.9 %custom-call.15 = f32[2,128,128]{1,2,0:T(8,128)S(1)} custom-call(f32[2,128,128]{2,1,0:T(8,128)S(1)} %get-tuple-element.18), custom_call_target="InvertDiagBlocksLowerTriangular" | custom-call | tf_op jit(solution)/shard_map/triangular_solve | solution.py:71
  380.2 3.1 fusion.17
  383.4 1.8 convolution_subtract_fusion
  385.2 1.7 convolution_convert_fusion
  386.9 1.1 pad_maximum_fusion
  (57 shorter events, 4.2 us)
Async XLA Ops:
  7.2 1.6 copy-start
  11.7 11.7 %all-to-all-start = ((f32[2,32,4,512]{3,2,1,0:T(4,128)}), f32[2,32,4,512]{3,2,1,0:T(4,128)S(1)}, u32[]{:S(2)}, u32[]{:S(2)}) async-start(f32[2,32,4,512]{3,2,1,0:T(4,128)} %bitcast.70), calls=%async_computation | async-start | bytes 1048576 | tf_op jit(solution)/shard_map/all_to_all | solution.py:17
  68.9 55.3 %all-to-all-start.4 = ((f32[8,256,256]{2,1,0:T(8,128)}), f32[8,256,256]{2,1,0:T(8,128)}, u32[]{:S(2)}, u32[]{:S(2)}) async-start(f32[8,256,256]{2,1,0:T(8,128)} %broadcast_in_dim.12), calls=%async_computation.4 | async-start | bytes 4194304 | tf_op jit(solution)/shard_map/all_to_all | solution.py:36
  75.8 191.3 %all-reduce.3.cloned.1.call-start = ((), (), s32[]{:S(2)}) async-start(), calls=%async_computation.9 | async-start | bytes 4112384 | tf_op jit(solution)/shard_map/psum | solution.py:87
  187.8 2.0 copy-start.2
  380.2 3.1 copy-start.1
Sparse Core Ops, SparseCore 0:
  190.0 77.0 all-reduce.2
where the time goes:
time: 399 us; the launch traced here: 395 us
  waiting for transfers between devices  126 us (32%)
  other arithmetic  112 us (28%)
  blocking collectives  87.3 us (22%)
  matrix products  19.1 us (5%)
  starting transfers between devices  17.5 us (4%)
  between operations  17.2 us (4%)
  local copies, waits for them, and re-layouts  15.3 us (4%)
    psum x1, waiting for transfers between devices, local(): z_total = lax.psum(z_part, 'row')  77.2 us
    another operation x13, other arithmetic, solve_rows(): lower = jnp.linalg.cholesky(gram)  68.7 us
    all_to_all x1, waiting for transfers between devices, copy_for_each(): lax.all_to_all(jnp.broadcast_to(array[None], (peers, *array.shape)), axis...  47.8 us
    all_to_all x4, blocking collectives, copy_for_each(): lax.all_to_all(jnp.broadcast_to(array[None], (peers, *array.shape)), axis...  41.7 us
    another operation x7, other arithmetic, solve_rows(): lax.linalg.triangular_solve(lower, block, left_side=True, lower=True)  40.7 us
    all_to_all x2, blocking collectives, summed_rows(): lax.all_to_all(nearer, far, split_axis=0, concat_axis=0, tiled=True)  37.9 us
    all_to_all x1, starting transfers between devices, sum_at_owner(): lax.all_to_all(in_blocks(array, dim, peers), axis, 0, 0, tiled=True)  10.4 us
    another operation x12, local copies, waits for them, and re-layouts  8.04 us
  transfers between devices with their start and end apart: 3, of which 3 were waited for; matrix products, arithmetic and copies ran while one was open for 0% of the time, Pallas kernels for 0%

commit v1 on v0

--- a/solution.py
+++ b/solution.py
@@ -84,7 +84,8 @@
     gram_left = of_everyone(local_gram(y_total), "row") / rows_total
     left = solve_rows(gram_left, y_total)
     z_part = jnp.dot(left, ppmi, preferred_element_type=jnp.float32)
-    z_total = lax.psum(z_part, "row")
+    parts = lax.all_gather(z_part, "row")
+    z_total = jnp.sum(parts, axis=0)
     gram_right = nested_sum(local_gram(z_total), (("col_0", "col_1"), "col_2")) / cols_total
     basis_now = solve_rows(gram_right, z_total)
     return (left, basis_now)

time: 399 us -> 507 us (1.27)
  waiting for transfers between devices: 126 us -> 214 us
  local copies, waits for them, and re-layouts: 15.3 us -> 31 us
  other arithmetic: 112 us -> 120 us
    all_gather x0 -> x1, waiting for transfers between devices: none -> 165 us  [local(): parts = lax.all_gather(z_part, 'row')]
    psum x1 -> x0, waiting for transfers between devices: 77.2 us -> none  [local(): z_total = lax.psum(z_part, 'row')]
    unnamed x8 -> x11, local copies, waits for them, and re-layouts: 1.61 us -> 12.5 us
    reduce_sum x0 -> x1, other arithmetic: none -> 8.61 us  [local(): z_total = jnp.sum(parts, axis=0)]
where the time goes in v1:
time: 507 us; the launch traced here: 503 us
  waiting for transfers between devices  214 us (42%)
  other arithmetic  120 us (24%)
  blocking collectives  84 us (17%)
  local copies, waits for them, and re-layouts  31 us (6%)
  matrix products  18 us (4%)
  starting transfers between devices  17.7 us (3%)
  between operations  17.2 us (3%)
    all_gather x1, waiting for transfers between devices, local(): parts = lax.all_gather(z_part, 'row')  165 us
    another operation x13, other arithmetic, solve_rows(): lower = jnp.linalg.cholesky(gram)  68.7 us
    all_to_all x1, waiting for transfers between devices, copy_for_each(): lax.all_to_all(jnp.broadcast_to(array[None], (peers, *array.shape)), axis...  47.6 us
    all_to_all x4, blocking collectives, copy_for_each(): lax.all_to_all(jnp.broadcast_to(array[None], (peers, *array.shape)), axis...  41.8 us
    another operation x7, other arithmetic, solve_rows(): lax.linalg.triangular_solve(lower, block, left_side=True, lower=True)  40.8 us
    all_to_all x2, blocking collectives, summed_rows(): lax.all_to_all(nearer, far, split_axis=0, concat_axis=0, tiled=True)  37.9 us
    unnamed x11, local copies, waits for them, and re-layouts  12.5 us
    all_to_all x1, starting transfers between devices, sum_at_owner(): lax.all_to_all(in_blocks(array, dim, peers), axis, 0, 0, tiled=True)  10.4 us
  transfers between devices with their start and end apart: 3, of which 3 were waited for; matrix products, arithmetic and copies ran while one was open for 0% of the time, Pallas kernels for 0%

profile of v1, /device:TPU:1, one launch (start us, length us, event | category | flops | bytes accessed | tf_op | source)
XLA Modules:
  0.0 502.8 jit_solution(8747175505193674600)
XLA Ops:
  7.2 1.6 copy-done
  8.7 1.9 fusion.26
  10.8 0.8 copy.60
  11.7 10.4 %all-to-all-start = ((f32[2,32,4,512]{3,2,1,0:T(4,128)}), f32[2,32,4,512]{3,2,1,0:T(4,128)S(1)}, u32[]{:S(2)}, u32[]{:S(2)}) async-start(f32[2,32,4,512]{3,2,1,0:T(4,128)} %bitcast.81), calls=%async_computation | async-start | bytes 1048576 | tf_op jit(solution)/shard_map/all_to_all | solution.py:17
  22.0 1.4 all-to-all-done
  23.6 18.9 %all_to_all.49 = f32[32,4,512]{2,1,0:T(4,128)S(1)} all-to-all(f32[32,4,512]{2,1,0:T(4,128)S(1)} %reduce_sum.54), channel_id=1, replica_groups=mesh['row'=8,'col_0'=8,'col_1'=4,'col_2'=2] {'col_0','col_1'}, dimensions={0} | all-to-all | bytes 524288 | tf_op jit(solution)/shard_map/all_to_all | solution.py:25
  42.6 15.0 %all_to_all.45 = f32[32,4,512]{2,1,0:T(4,128)S(1)} all-to-all(f32[32,4,512]{2,1,0:T(4,128)S(1)} %broadcast_in_dim.10), channel_id=1, replica_groups=mesh['row'=8,'col_0'=8,'col_1'=4,'col_2'=2] {'col_0','col_1'}, dimensions={0} | all-to-all | bytes 524288 | tf_op jit(solution)/shard_map/all_to_all | solution.py:36
  57.7 7.1 %all_to_all.46 = f32[2,32,4,512]{3,2,1,0:T(4,128)S(1)} all-to-all(f32[2,32,4,512]{3,2,1,0:T(4,128)S(1)} %broadcast_in_dim.11), channel_id=1, replica_groups=mesh['row'=8,'col_0'=8,'col_1'=4,'col_2'=2] {'col_2'}, dimensions={0} | all-to-all | bytes 1048576 | tf_op jit(solution)/shard_map/all_to_all | solution.py:36
  64.7 0.9 copy.42
  65.6 1.2 reshape_reshape.9
  67.5 1.5 broadcast_in_dim.12
  68.9 6.8 %all-to-all-start.4 = ((f32[8,256,256]{2,1,0:T(8,128)}), f32[8,256,256]{2,1,0:T(8,128)}, u32[]{:S(2)}, u32[]{:S(2)}) async-start(f32[8,256,256]{2,1,0:T(8,128)} %broadcast_in_dim.12), calls=%async_computation.4 | async-start | bytes 4194304 | tf_op jit(solution)/shard_map/all_to_all | solution.py:36
  76.6 47.6 %all-to-all-done.4 = f32[8,256,256]{2,1,0:T(8,128)} async-done(((f32[8,256,256]{2,1,0:T(8,128)}), f32[8,256,256]{2,1,0:T(8,128)}, u32[]{:S(2)}, u32[]{:S(2)}) %all-to-all-start.4) | async-done | bytes 2097184 | tf_op jit(solution)/shard_map/all_to_all | solution.py:36
  124.2 1.8 reduce_sum.56
  126.3 11.7 %cholesky.130 = f32[128,128]{1,0:T(8,128)S(1)} custom-call(f32[128,128]{1,0:T(8,128)S(1)} %cholesky.194), custom_call_target="Cholesky" | custom-call | tf_op jit(solution)/shard_map/jit(cholesky)/cholesky | solution.py:70
  138.1 9.8 %custom-call.17 = f32[1,128,128]{1,2,0:T(8,128)S(1)} custom-call(f32[1,128,128]{2,1,0:T(8,128)S(1)} %get-tuple-element.48), custom_call_target="InvertDiagBlocksLowerTriangular" | custom-call | tf_op jit(solution)/shard_map/jit(cholesky)/cholesky | solution.py:70
  148.4 11.7 %cholesky.147 = f32[128,128]{1,0:T(8,128)S(1)} custom-call(f32[128,128]{1,0:T(8,128)S(1)} %convolution_subtract_fusion.3), custom_call_target="Cholesky" | custom-call | tf_op jit(solution)/shard_map/jit(cholesky)/cholesky | solution.py:70
  160.1 0.7 compare_reduce_fusion.2
  162.2 4.2 while.2
  162.4 0.7 fusion.46
  163.1 1.3 bitcast_dynamic-update-slice_fusion.4
  164.5 0.7 fusion.46
  165.1 1.3 bitcast_dynamic-update-slice_fusion.4
  166.5 19.7 %custom-call.14 = f32[2,128,128]{1,2,0:T(8,128)S(1)} custom-call(f32[2,128,128]{2,1,0:T(8,128)S(1)} %get-tuple-element.10), custom_call_target="InvertDiagBlocksLowerTriangular" | custom-call | tf_op jit(solution)/shard_map/triangular_solve | solution.py:71
  187.4 2.0 fusion.28
  189.5 165.4 %all-gather.3.cloned.1.call-done = f32[2048,2004]{0,1:T(8,128)} async-done(((f32[256,2004]{0,1:T(8,128)}), f32[2048,2004]{0,1:T(8,128)}) %all-gather.3.cloned.1.call-update) | async-done | bytes 16416784 | tf_op jit(solution)/shard_map/all_gather | solution.py:87
  354.9 10.9 %copy.54 = f32[251,8,8,256]{3,2,1,0:T(8,128)S(1)} copy(f32[251,8,8,256]{3,1,2,0:T(8,128)} %bitcast.95) | data formatting | bytes 32899072
  365.8 8.6 %bitcast_reduce_fusion = f32[256,2004]{0,1:T(8,128)S(1)} fusion(f32[2008,8,256]{2,1,0:T(8,128)S(1)} %bitcast.94), kind=kLoop, calls=%fused_computation.4 | loop fusion | flops 3591168 | bytes 18468864 | tf_op jit(solution)/shard_map/reduce_sum | solution.py:88
  374.4 2.0 copy.47
  376.4 2.9 dot_general.17
  379.2 4.6 fusion.3
  383.8 4.3 all_to_all.47
  388.2 19.1 %all_to_all.50 = f32[32,4,256]{2,1,0:T(4,128)S(1)} all-to-all(f32[32,4,256]{2,1,0:T(4,128)S(1)} %copy.49), channel_id=1, replica_groups=mesh['row'=8,'col_0'=8,'col_1'=4,'col_2'=2] {'col_0','col_1'}, dimensions={0} | all-to-all | bytes 262144 | tf_op jit(solution)/shard_map/all_to_all | solution.py:25
  407.3 13.0 %all_to_all.51 = f32[32,4,256]{2,1,0:T(4,128)S(1)} all-to-all(f32[32,4,256]{2,1,0:T(4,128)S(1)} %broadcast_in_dim.14), channel_id=1, replica_groups=mesh['row'=8,'col_0'=8,'col_1'=4,'col_2'=2] {'col_0','col_1'}, dimensions={0} | all-to-all | bytes 262144 | tf_op jit(solution)/shard_map/all_to_all | solution.py:36
  420.4 6.7 %all_to_all.48 = f32[2,32,4,256]{3,2,1,0:T(4,128)S(1)} all-to-all(f32[2,32,4,256]{3,2,1,0:T(4,128)S(1)} %broadcast_in_dim.15), channel_id=1, replica_groups=mesh['row'=8,'col_0'=8,'col_1'=4,'col_2'=2] {'col_2'}, dimensions={0} | all-to-all | bytes 524288 | tf_op jit(solution)/shard_map/all_to_all | solution.py:36
  427.4 11.7 %cholesky.164 = f32[128,128]{1,0:T(8,128)S(1)} custom-call(f32[128,128]{1,0:T(8,128)S(1)} %cholesky.197), custom_call_target="Cholesky" | custom-call | tf_op jit(solution)/shard_map/jit(cholesky)/cholesky | solution.py:70
  439.2 9.8 %custom-call.18 = f32[1,128,128]{1,2,0:T(8,128)S(1)} custom-call(f32[1,128,128]{2,1,0:T(8,128)S(1)} %get-tuple-element.44), custom_call_target="InvertDiagBlocksLowerTriangular" | custom-call | tf_op jit(solution)/shard_map/jit(cholesky)/cholesky | solution.py:70
  449.5 11.7 %cholesky.181 = f32[128,128]{1,0:T(8,128)S(1)} custom-call(f32[128,128]{1,0:T(8,128)S(1)} %convolution_subtract_fusion.2), custom_call_target="Cholesky" | custom-call | tf_op jit(solution)/shard_map/jit(cholesky)/cholesky | solution.py:70
  461.9 0.7 compare_reduce_fusion.1
  463.9 4.1 while.3
  463.9 0.7 fusion.47
  464.6 1.3 bitcast_dynamic-update-slice_fusion.5
  466.6 1.3 bitcast_dynamic-update-slice_fusion.5
  468.0 19.9 %custom-call.15 = f32[2,128,128]{1,2,0:T(8,128)S(1)} custom-call(f32[2,128,128]{2,1,0:T(8,128)S(1)} %get-tuple-element.18), custom_call_target="InvertDiagBlocksLowerTriangular" | custom-call | tf_op jit(solution)/shard_map/triangular_solve | solution.py:71
  487.9 1.8 fusion.25
  489.7 3.1 convolution_subtract_fusion
  492.8 1.8 convolution_convert_fusion
  494.6 1.1 pad_maximum_fusion
  (62 shorter events, 6.7 us)
Async XLA Ops:
  7.2 1.6 copy-start
  11.7 11.7 %all-to-all-start = ((f32[2,32,4,512]{3,2,1,0:T(4,128)}), f32[2,32,4,512]{3,2,1,0:T(4,128)S(1)}, u32[]{:S(2)}, u32[]{:S(2)}) async-start(f32[2,32,4,512]{3,2,1,0:T(4,128)} %bitcast.81), calls=%async_computation | async-start | bytes 1048576 | tf_op jit(solution)/shard_map/all_to_all | solution.py:17
  68.9 55.3 %all-to-all-start.4 = ((f32[8,256,256]{2,1,0:T(8,128)}), f32[8,256,256]{2,1,0:T(8,128)}, u32[]{:S(2)}, u32[]{:S(2)}) async-start(f32[8,256,256]{2,1,0:T(8,128)} %broadcast_in_dim.12), calls=%async_computation.4 | async-start | bytes 4194304 | tf_op jit(solution)/shard_map/all_to_all | solution.py:36
  75.8 279.1 %all-gather.3.cloned.1.call-start = ((), (), s32[]{:S(2)}) async-start(), calls=%async_computation.9 | async-start | bytes 18505728 | tf_op jit(solution)/shard_map/all_gather | solution.py:87
  187.4 2.1 copy-start.3
  374.4 113.5 %copy-start.2 = (f32[256,2004]{0,1:T(8,128)}, f32[256,2004]{0,1:T(8,128)S(1)}, u32[]{:S(2)}) copy-start(f32[256,2004]{0,1:T(8,128)S(1)} %bitcast_reduce_fusion) | copy-start | bytes 6156292
  489.7 6.0 %copy-start.1 = (bf16[512,2004]{0,1:T(8,128)(2,1)S(1)}, bf16[512,2004]{0,1:T(8,128)(2,1)}, u32[]{:S(2)}) copy-start(bf16[512,2004]{0,1:T(8,128)(2,1)} %param.3) | copy-start | bytes 6156292
Sparse Core Ops, SparseCore 0:
  189.6 165.2 all-gather.2
